TPU v7x, 128 devices: a whole 4x4x4 slice. The times are simulated.
128 devices in a mesh: freq: 8 (over y, z_lo), rows: 16 (over z_hi, x, core).
Axes of the slice: x: 4, y: 4, z: 4 (z_hi: 2, z_lo: 2; z = z_hi * 2 + z_lo), core: 2. Of those that a mesh axis runs over, the one named last changes fastest.
Arguments:
- refl: bfloat16 [2, 16, 4608, 4608], P(None, 'freq', 'rows'), may hold values from -0.125 to 0.125
- refl_scale: float32 [16, 4608, 36], P('freq', 'rows'), may hold values from 0.5 to 4
- focus: bfloat16 [16, 4608, 128], P('freq', 'rows'), may hold values from -6 to 6
- first_mute: int32 [4608, 64], P('rows'), may hold values from 128 to 1023
- second_mute: int32 [64, 4608], P('freq', 'rows'), may hold values from 256 to 1023
Outputs:
- focus_next: float32 [64, 4608, 1024], P('freq', 'rows')
All inputs are finite; a program needn't handle non-finite values.
Results may differ from a plain program's by a relative error of at most 0.0085.
Values may be sent and summed in bfloat16 or wider, within the bound.
No kernel may reach another device: no remote copies, remote signals or barrier semaphores. Data moves between devices by JAX's collectives and lax.ppermute only.
A program may use at most 128 MiB of HBM per device.

v0:
```python
import math
import jax
import jax.numpy as jnp
from jax import lax
from jax.sharding import PartitionSpec as P

NT = 1024
LOWBIN = 24


def tables(freq_total):
    time_index = jnp.arange(NT, dtype=jnp.int32)
    freq_bins = LOWBIN + jnp.arange(freq_total, dtype=jnp.int32)
    phases = (freq_bins[:, None] * time_index[None, :] % NT).astype(jnp.float32) * (
        2.0 * math.pi / NT
    )
    inward = 1.0 / math.sqrt(2.0 * freq_total)
    outward = 2.0 / (NT * inward)
    basis_rows = jnp.concatenate([jnp.cos(phases), -jnp.sin(phases)], 0)
    return (basis_rows.T * inward, basis_rows * outward)


def split_basis(basis):
    upper = basis.astype(jnp.bfloat16)
    lower = (basis - upper.astype(jnp.float32)).astype(jnp.bfloat16)
    return (upper, lower)


def decode(quantized, block_scale):
    blocks = block_scale.shape[-1]
    reshaped = quantized.reshape(quantized.shape[:3] + (blocks, quantized.shape[3] // blocks))
    return (
        (reshaped * block_scale[None, :, :, :, None]).astype(jnp.bfloat16).reshape(quantized.shape)
    )


def combine_first(direct, crossed, points):
    return jnp.concatenate(
        [
            direct[..., :points] - crossed[..., points:],
            direct[..., points:] + crossed[..., :points],
        ],
        -1,
    )


def combine_second(direct, crossed, points):
    return jnp.concatenate(
        [
            direct[..., :points] + crossed[..., points:],
            direct[..., points:] - crossed[..., :points],
        ],
        -1,
    )


def mute_pass(samples, cutoff, inverse, forward):
    upper, lower = split_basis(inverse)
    traces = jnp.dot(upper, samples, preferred_element_type=jnp.float32) + jnp.dot(
        lower, samples, preferred_element_type=jnp.float32
    )
    time_index = jnp.arange(NT, dtype=jnp.int32)
    kept = jnp.where(time_index[:, None] < cutoff[None, :], traces, 0.0)
    return jnp.dot(forward, kept, precision=lax.Precision.HIGHEST).astype(jnp.bfloat16)


def on_device(refl, refl_scale, focus, first_mute, second_mute):
    groups = lax.axis_size("freq")
    freq_dev = refl.shape[1]
    rows_dev = refl.shape[2]
    points = focus.shape[2] // 2
    freq_total = freq_dev * groups
    inverse, forward = tables(freq_total)
    decoded = decode(refl, refl_scale)
    columns = decoded
    paired = jnp.einsum(
        "kfsn,fnc->kfsc",
        columns,
        lax.all_gather(focus, "rows", axis=1, tiled=True),
        preferred_element_type=jnp.float32,
    )
    focused = combine_first(paired[0], paired[1], points).astype(jnp.bfloat16)
    self_index = lax.axis_index("freq")
    block_size = points // groups
    exchanged = lax.all_to_all(
        focused.reshape(freq_dev, rows_dev, 2, points),
        "freq",
        split_axis=3,
        concat_axis=0,
        tiled=True,
    )
    samples = exchanged.transpose(2, 0, 1, 3).reshape(2 * freq_total, rows_dev * block_size)
    cutoff = lax.dynamic_slice_in_dim(first_mute, self_index * block_size, block_size, 1).reshape(
        rows_dev * block_size
    )
    spectra = mute_pass(samples, cutoff, inverse, forward)
    spectra = spectra.reshape(2, freq_total, rows_dev, block_size).transpose(1, 2, 0, 3)
    returned = lax.all_to_all(spectra, "freq", split_axis=0, concat_axis=3, tiled=True).reshape(
        freq_dev, rows_dev, 2 * points
    )
    point_share = points // groups
    columns = decoded
    products = jnp.einsum("kfsn,fsc->knfc", columns, returned, preferred_element_type=jnp.float32)
    summed = lax.psum_scatter(
        combine_second(products[0], products[1], points), "rows", scatter_dimension=0, tiled=True
    )
    adjoint_half = summed.astype(jnp.bfloat16).reshape(rows_dev, freq_dev, 2, points)
    regrouped = lax.all_to_all(adjoint_half, "freq", split_axis=3, concat_axis=1, tiled=True)
    final_samples = regrouped.transpose(3, 0, 2, 1).reshape(point_share * rows_dev, 2 * freq_total)
    upper, lower = split_basis(inverse.T)
    traces = jnp.dot(final_samples, upper, preferred_element_type=jnp.float32) + jnp.dot(
        final_samples, lower, preferred_element_type=jnp.float32
    )
    traces = traces.reshape(point_share, rows_dev, NT)
    time_index = jnp.arange(NT, dtype=jnp.int32)
    return jnp.where(time_index[None, None, :] < second_mute[:, :, None], traces, 0.0)


def solution(mesh):
    in_specs = (
        P(None, "freq", "rows", None),
        P("freq", "rows", None),
        P("freq", "rows", None),
        P("rows", None),
        P("freq", "rows"),
    )
    out_specs = P("freq", "rows", None)
    return jax.shard_map(
        on_device, mesh=mesh, in_specs=in_specs, out_specs=out_specs, check_vma=False
    )
```

profile of v0, /device:TPU:0, one launch (start us, length us, event | category | flops | bytes accessed | tf_op | source)
XLA Modules:
  0.0 245.4 jit_solution(14717921745920987155)
XLA Ops:
  6.5 0.7 all-gather.2.cloned.1.call-update
  7.3 1.0 copy.60
  8.3 6.3 %mul.70 = f32[2,288,36,128]{3,2,1,0:T(8,128)} broadcast(f32[2,288,36]{2,1,0:T(8,128)S(1)} %copy.60), dimensions={0,1,2} | broadcast | bytes 10699776 | tf_op jit(solution)/shard_map/mul | solution.py:33
  14.6 12.4 %mul.71 = f32[2,288,4608]{2,1,0:T(8,128)} reshape(f32[2,288,36,128]{3,2,1,0:T(8,128)} %mul.70) | data formatting | bytes 21233664 | tf_op jit(solution)/shard_map/mul | solution.py:33
  27.2 34.3 %all-gather.2.cloned.1.call-done = bf16[2,4608,128]{2,1,0:T(8,128)(2,1)} async-done(((bf16[2,288,128]{2,1,0:T(8,128)(2,1)}), bf16[2,4608,128]{2,1,0:T(8,128)(2,1)}) %all-gather.2.cloned.1.call-update) | async-done | bytes 2359312 | tf_op jit(solution)/shard_map/all_gather | solution.py:79
  61.5 9.3 %fusion.17 = f32[2,2,288,128]{3,2,0,1:T(8,128)S(1)} fusion(bf16[2,4608,128]{2,1,0:T(8,128)(2,1)} %all-gather.2.cloned.1.call-done, bf16[2,2,288,4608]{3,2,1,0:T(8,128)(2,1)} %param.5, f32[2,288,4608]{2,1,0:T(8,128)} %mul.71), kind=kOutput, calls=%fused_computation.22 | convolution fusion | flops 1374879744 | bytes 24182784 | tf_op jit(solution)/shard_map/kfsn,fnc->kfsc/dot_general | solution.py:76
  71.2 0.9 copy.63
  72.1 4.4 %all-to-all-start = ((bf16[2,288,2,64]{1,2,0,3:T(2,128)(2,1)}), bf16[2,288,2,64]{1,2,0,3:T(2,128)(2,1)S(1)}, u32[]{:S(2)}, u32[]{:S(2)}) async-start(bf16[2,288,2,64]{1,2,0,3:T(2,128)(2,1)} %copy.63), calls=%async_computation | async-start | bytes 393216 | tf_op jit(solution)/shard_map/all_to_all | solution.py:85
  76.8 6.6 %all-to-all-done = bf16[2,288,2,64]{1,2,0,3:T(2,128)(2,1)S(1)} async-done(((bf16[2,288,2,64]{1,2,0,3:T(2,128)(2,1)}), bf16[2,288,2,64]{1,2,0,3:T(2,128)(2,1)S(1)}, u32[]{:S(2)}, u32[]{:S(2)}) %all-to-all-start) | async-done | bytes 147488 | tf_op jit(solution)/shard_map/all_to_all | solution.py:85
  83.4 1.6 copy.66
  85.6 1.4 fusion.32
  87.1 1.4 fusion.44
  88.5 6.4 %fusion.13 = bf16[32,2304]{1,0:T(8,128)(2,1)S(1)} fusion(f32[1024,2304]{1,0:T(8,128)S(1)} %fusion.44, f32[1024,2304]{1,0:T(8,128)S(1)} %fusion.32, s32[2304]{0:T(1024)S(1)} %lt.45, f32[16,1024]{1,0:T(8,128)S(1)} %get-tuple-element.14, f32[16,1024]{1,0:T(8,128)S(1)} %get-tuple-element.13), kind=kOutput, calls=%fused_computation.18 | convolution fusion | flops 913186816 | bytes 19162112 | tf_op jit(solution)/shard_map/dot_general | solution.py:64
  95.7 2.3 copy.68
  98.0 3.6 %all-to-all-start.1 = ((bf16[16,288,2,8]{1,3,2,0:T(8,128)(2,1)}), bf16[16,288,2,8]{1,3,2,0:T(8,128)(2,1)S(1)}, u32[]{:S(2)}, u32[]{:S(2)}) async-start(bf16[16,288,2,8]{1,3,2,0:T(8,128)(2,1)} %copy.68), calls=%async_computation.1 | async-start | bytes 393216 | tf_op jit(solution)/shard_map/all_to_all | solution.py:98
  102.8 5.2 %all-to-all-done.1 = bf16[16,288,2,8]{1,3,2,0:T(8,128)(2,1)S(1)} async-done(((bf16[16,288,2,8]{1,3,2,0:T(8,128)(2,1)}), bf16[16,288,2,8]{1,3,2,0:T(8,128)(2,1)S(1)}, u32[]{:S(2)}, u32[]{:S(2)}) %all-to-all-start.1) | async-done | bytes 147488 | tf_op jit(solution)/shard_map/all_to_all | solution.py:98
  108.0 8.6 %fusion.8 = f32[2,4608,2,128]{1,3,0,2:T(8,128)S(1)} fusion(bf16[2,288,128,1]{1,2,3,0:T(8,128)(2,1)S(1)} %bitcast.80, bf16[2,2,288,4608]{3,2,1,0:T(8,128)(2,1)} %param.5, f32[2,288,4608]{2,1,0:T(8,128)} %mul.71), kind=kOutput, calls=%fused_computation.11 | convolution fusion | flops 1374879744 | bytes 30818304 | tf_op jit(solution)/shard_map/kfsn,fsc->knfc/dot_general | solution.py:103
  117.8 2.5 %pad_maximum_fusion = f32[4608,2,128]{0,2,1:T(8,128)} fusion(f32[4608,2,64]{0,2,1:T(8,128)S(1)} %get-tuple-element.6, f32[4608,2,64]{0,2,1:T(8,128)S(1)} %get-tuple-element.5), kind=kLoop, calls=%fused_computation.15 | loop fusion | flops 1179648 | bytes 9437184 | tf_op jit(solution)/shard_map/concatenate | solution.py:48
  120.3 8.0 %copy.73 = f32[4608,2,128]{2,1,0:T(2,128)} copy(f32[4608,2,128]{0,2,1:T(8,128)} %pad_maximum_fusion) | data formatting | bytes 9437184 | tf_op jit(solution)/shard_map/concatenate | solution.py:48
  128.4 93.2 %all-reduce.2 = bf16[4608,2,128]{2,1,0:T(2,128)(2,1)S(1)} all-reduce(f32[4608,2,128]{2,1,0:T(2,128)} %copy.73), channel_id=2, replica_groups=mesh['freq'=8,'rows'=16] {'rows'}, use_global_device_ids=true, to_apply=%region_0.1.clone | all-reduce | flops 1179648 | bytes 7077888
  222.1 9.2 %all_to_all.51 = bf16[288,2,2,64]{0,2,1,3:T(2,128)(2,1)S(1)} all-to-all(bf16[288,2,2,64]{0,2,1,3:T(2,128)(2,1)S(1)} %copy.75), channel_id=1, replica_groups=mesh['freq'=8,'rows'=16] {'freq'}, dimensions={3} | all-to-all | bytes 294912 | tf_op jit(solution)/shard_map/all_to_all | solution.py:108
  231.5 1.4 fusion.42
  233.0 1.4 convolution_add_fusion
  234.4 4.2 %fusion.3 = f32[8,288,1024]{2,1,0:T(8,128)} fusion(f32[8,288,1024]{2,1,0:T(8,128)S(1)} %bitcast.78, s32[8,288]{1,0:T(8,128)S(1)} %copy-done.2), kind=kLoop, calls=%fused_computation.6 | loop fusion | flops 4718592 | bytes 18883584 | tf_op jit(solution)/shard_map/jit(_where)/select_n | solution.py:116
  (33 shorter events, 4.8 us)
Async XLA Ops:
  6.5 20.4 %copy-start = (s32[288,64]{0,1:T(8,128)S(1)}, s32[288,64]{0,1:T(8,128)}, u32[]{:S(2)}) copy-start(s32[288,64]{0,1:T(8,128)} %param.8) | copy-start | bytes 221188
  6.5 55.0 %all-gather.2.cloned.1.call-start = ((), (), s32[]{:S(2)}) async-start(), calls=%async_computation.3 | async-start | bytes 2506752 | tf_op jit(solution)/shard_map/all_gather | solution.py:79
  72.1 11.3 %all-to-all-start = ((bf16[2,288,2,64]{1,2,0,3:T(2,128)(2,1)}), bf16[2,288,2,64]{1,2,0,3:T(2,128)(2,1)S(1)}, u32[]{:S(2)}, u32[]{:S(2)}) async-start(bf16[2,288,2,64]{1,2,0,3:T(2,128)(2,1)} %copy.63), calls=%async_computation | async-start | bytes 393216 | tf_op jit(solution)/shard_map/all_to_all | solution.py:85
  88.5 13.1 %copy-start.3 = (u32[128]{0:T(128)S(1)}, u32[128]{0:T(128)}, u32[]{:S(2)}) copy-start(u32[128]{0:T(128)} %constant.41) | copy-start | bytes 1540
  98.0 10.0 %all-to-all-start.1 = ((bf16[16,288,2,8]{1,3,2,0:T(8,128)(2,1)}), bf16[16,288,2,8]{1,3,2,0:T(8,128)(2,1)S(1)}, u32[]{:S(2)}, u32[]{:S(2)}) async-start(bf16[16,288,2,8]{1,3,2,0:T(8,128)(2,1)} %copy.68), calls=%async_computation.1 | async-start | bytes 393216 | tf_op jit(solution)/shard_map/all_to_all | solution.py:98
  232.9 1.4 copy-start.2
  234.4 4.2 %copy-start.1 = (s32[288,64]{0,1:T(8,128)S(1)}, s32[288,64]{0,1:T(8,128)}, u32[]{:S(2)}) copy-start(s32[288,64]{0,1:T(8,128)} %param.8) | copy-start | bytes 221188
Sparse Core Ops, SparseCore 0:
  9.8 51.6 all-gather.1
where the time goes:
time: 246 us; the launch traced here: 245 us
  blocking collectives  102 us (41%)
  waiting for transfers between devices  46.8 us (19%)
  local copies, waits for them, and re-layouts  36.1 us (15%)
  matrix products  30.1 us (12%)
  between operations  14.2 us (6%)
  starting transfers between devices  7.99 us (3%)
  other arithmetic  7.83 us (3%)
    unnamed x1, blocking collectives  93.2 us
    all_gather x1, waiting for transfers between devices, on_device(): lax.all_gather(focus, 'rows', axis=1, tiled=True)  34.3 us
    mul x2, local copies, waits for them, and re-layouts, decode(): reshaped * block_scale[None, :, :, :, None]  18.7 us
    dot_general x1, matrix products, on_device(): jnp.einsum('kfsn,fnc->kfsc', columns, lax.all_gather(focus, 'rows', axis=...  9.34 us
    all_to_all x1, blocking collectives, on_device(): lax.all_to_all(adjoint_half, 'freq', split_axis=3, concat_axis=1, tiled=T...  9.18 us
    dot_general x1, matrix products, on_device(): jnp.einsum('kfsn,fsc->knfc', columns, returned, preferred_element_type=jn...  8.6 us
    concatenate x1, local copies, waits for them, and re-layouts, combine_second(): jnp.concatenate([direct[..., :points] + crossed[..., points:], direct[......  8.04 us
    all_to_all x1, waiting for transfers between devices, on_device(): lax.all_to_all(focused.reshape(freq_dev, rows_dev, 2, points), 'freq', sp...  6.59 us
  transfers between devices with their start and end apart: 3, of which 3 were waited for; matrix products, arithmetic and copies ran while one was open for 9% of the time, Pallas kernels for 0%

commit v1 on v0

--- a/solution.py
+++ b/solution.py
@@ -6,6 +6,18 @@
 
 NT = 1024
 LOWBIN = 24
+
+
+def detail_waves(which_axis, u_in):
+    return jnp.concatenate(
+        lax.all_to_all(
+            jnp.stack(lax.psum(1, axis_name=which_axis) * [u_in], 0),
+            axis_name=which_axis,
+            split_axis=0,
+            concat_axis=0,
+        ),
+        1,
+    )
 
 
 def tables(freq_total):
@@ -74,10 +86,7 @@
     decoded = decode(refl, refl_scale)
     columns = decoded
     paired = jnp.einsum(
-        "kfsn,fnc->kfsc",
-        columns,
-        lax.all_gather(focus, "rows", axis=1, tiled=True),
-        preferred_element_type=jnp.float32,
+        "kfsn,fnc->kfsc", columns, detail_waves("rows", focus), preferred_element_type=jnp.float32
     )
     focused = combine_first(paired[0], paired[1], points).astype(jnp.bfloat16)
     self_index = lax.axis_index("freq")

time: 246 us -> 220 us (0.89)
  waiting for transfers between devices: 46.8 us -> 23.5 us
  between operations: 14.2 us -> 0.92 us
  starting transfers between devices: 7.99 us -> 16.4 us
  local copies, waits for them, and re-layouts: 36.1 us -> 39.1 us
    all_gather x1 -> x0, waiting for transfers between devices: 34.3 us -> none  [on_device(): lax.all_gather(focus, 'rows', axis=1, tiled=True)]
    all_to_all x0 -> x1, waiting for transfers between devices: none -> 12 us  [detail_waves(): lax.all_to_all(jnp.stack(lax.psum(1, axis_name=which_axis) * [u_in], 0),...]
    all_to_all x0 -> x1, starting transfers between devices: none -> 7.83 us  [detail_waves(): lax.all_to_all(jnp.stack(lax.psum(1, axis_name=which_axis) * [u_in], 0),...]
    another operation x0 -> x1, local copies, waits for them, and re-layouts: none -> 2.8 us  [detail_waves(): jnp.stack(lax.psum(1, axis_name=which_axis) * [u_in], 0)]
  transfers between devices with their start and end apart: 3 -> 3, of which waited for: 3 -> 3; matrix products, arithmetic and copies ran while one was open for 9% -> 10% of each run, Pallas kernels for 0% -> 0%
where the time goes in v1:
time: 220 us; the launch traced here: 219 us
  blocking collectives  102 us (46%)
  local copies, waits for them, and re-layouts  39.1 us (18%)
  matrix products  29.4 us (13%)
  waiting for transfers between devices  23.5 us (11%)
  starting transfers between devices  16.4 us (7%)
  other arithmetic  7.83 us (4%)
    unnamed x1, blocking collectives  92.7 us
    mul x2, local copies, waits for them, and re-layouts, decode(): reshaped * block_scale[None, :, :, :, None]  18.6 us
    all_to_all x1, waiting for transfers between devices, detail_waves(): lax.all_to_all(jnp.stack(lax.psum(1, axis_name=which_axis) * [u_in], 0),...  12 us
    all_to_all x1, blocking collectives, on_device(): lax.all_to_all(adjoint_half, 'freq', split_axis=3, concat_axis=1, tiled=T...  9.44 us
    dot_general x1, matrix products, on_device(): jnp.einsum('kfsn,fnc->kfsc', columns, detail_waves('rows', focus), prefer...  8.74 us
    dot_general x1, matrix products, on_device(): jnp.einsum('kfsn,fsc->knfc', columns, returned, preferred_element_type=jn...  8.6 us
    concatenate x1, local copies, waits for them, and re-layouts, combine_second(): jnp.concatenate([direct[..., :points] + crossed[..., points:], direct[......  8.05 us
    all_to_all x1, starting transfers between devices, detail_waves(): lax.all_to_all(jnp.stack(lax.psum(1, axis_name=which_axis) * [u_in], 0),...  7.83 us
  transfers between devices with their start and end apart: 3, of which 3 were waited for; matrix products, arithmetic and copies ran while one was open for 10% of the time, Pallas kernels for 0%

profile of v1, /device:TPU:0, one launch (start us, length us, event | category | flops | bytes accessed | tf_op | source)
XLA Modules:
  0.0 219.3 jit_solution(14663069467446629712)
XLA Ops:
  0.0 2.8 %stack.2 = bf16[16,2,288,128]{3,2,1,0:T(8,128)(2,1)} broadcast(bf16[2,288,128]{2,1,0:T(8,128)(2,1)} %param.7), dimensions={1,2,3} | broadcast | bytes 2506752 | tf_op jit(solution)/shard_map/stack | solution.py:14
  2.8 7.8 %all-to-all-start = ((bf16[16,2,288,128]{3,2,1,0:T(8,128)(2,1)}), bf16[16,2,288,128]{3,2,1,0:T(8,128)(2,1)S(1)}, u32[]{:S(2)}, u32[]{:S(2)}) async-start(bf16[16,2,288,128]{3,2,1,0:T(8,128)(2,1)} %stack.2), calls=%async_computation | async-start | bytes 4718592 | tf_op jit(solution)/shard_map/all_to_all | solution.py:13
  10.6 1.0 copy.61
  11.7 6.3 %mul.70 = f32[2,288,36,128]{3,2,1,0:T(8,128)} broadcast(f32[2,288,36]{2,1,0:T(8,128)S(1)} %copy.61), dimensions={0,1,2} | broadcast | bytes 10699776 | tf_op jit(solution)/shard_map/mul | solution.py:45
  18.0 12.4 %mul.71 = f32[2,288,4608]{2,1,0:T(8,128)} reshape(f32[2,288,36,128]{3,2,1,0:T(8,128)} %mul.70) | data formatting | bytes 21233664 | tf_op jit(solution)/shard_map/mul | solution.py:45
  30.6 12.0 %all-to-all-done = bf16[16,2,288,128]{3,2,1,0:T(8,128)(2,1)S(1)} async-done(((bf16[16,2,288,128]{3,2,1,0:T(8,128)(2,1)}), bf16[16,2,288,128]{3,2,1,0:T(8,128)(2,1)S(1)}, u32[]{:S(2)}, u32[]{:S(2)}) %all-to-all-start) | async-done | bytes 2359328 | tf_op jit(solution)/shard_map/all_to_all | solution.py:13
  42.8 8.7 %fusion.16 = f32[2,2,288,128]{3,2,0,1:T(8,128)S(1)} fusion(bf16[2,4608,128,1]{2,1,3,0:T(8,128)(2,1)S(1)} %bitcast.79, bf16[2,2,288,4608]{3,2,1,0:T(8,128)(2,1)} %param.5, f32[2,288,4608]{2,1,0:T(8,128)} %mul.71), kind=kOutput, calls=%fused_computation.21 | convolution fusion | flops 1374879744 | bytes 24182784 | tf_op jit(solution)/shard_map/kfsn,fnc->kfsc/dot_general | solution.py:88
  52.8 4.9 %all-to-all-start.1 = ((bf16[2,288,2,64]{1,2,0,3:T(2,128)(2,1)}), bf16[2,288,2,64]{1,2,0,3:T(2,128)(2,1)S(1)}, u32[]{:S(2)}, u32[]{:S(2)}) async-start(bf16[2,288,2,64]{1,2,0,3:T(2,128)(2,1)} %copy.65), calls=%async_computation.1 | async-start | bytes 393216 | tf_op jit(solution)/shard_map/all_to_all | solution.py:94
  58.0 6.3 %all-to-all-done.1 = bf16[2,288,2,64]{1,2,0,3:T(2,128)(2,1)S(1)} async-done(((bf16[2,288,2,64]{1,2,0,3:T(2,128)(2,1)}), bf16[2,288,2,64]{1,2,0,3:T(2,128)(2,1)S(1)}, u32[]{:S(2)}, u32[]{:S(2)}) %all-to-all-start.1) | async-done | bytes 147488 | tf_op jit(solution)/shard_map/all_to_all | solution.py:94
  64.4 1.6 copy.68
  66.6 1.4 fusion.29
  68.0 1.4 fusion.41
  69.5 6.4 %fusion.13 = bf16[32,2304]{1,0:T(8,128)(2,1)S(1)} fusion(f32[1024,2304]{1,0:T(8,128)S(1)} %fusion.41, f32[1024,2304]{1,0:T(8,128)S(1)} %fusion.29, s32[2304]{0:T(1024)S(1)} %lt.45, f32[16,1024]{1,0:T(8,128)S(1)} %get-tuple-element.14, f32[16,1024]{1,0:T(8,128)S(1)} %get-tuple-element.13), kind=kOutput, calls=%fused_computation.18 | convolution fusion | flops 913186816 | bytes 19162112 | tf_op jit(solution)/shard_map/dot_general | solution.py:76
  76.7 2.3 %copy.70 = bf16[16,288,2,8]{1,3,2,0:T(8,128)(2,1)} copy(bf16[16,288,2,8]{0,2,3,1:T(2,128)(2,1)S(1)} %bitcast.81) | data formatting | bytes 294912 | tf_op jit(solution)/shard_map/transpose | solution.py:106
  79.0 3.6 %all-to-all-start.2 = ((bf16[16,288,2,8]{1,3,2,0:T(8,128)(2,1)}), bf16[16,288,2,8]{1,3,2,0:T(8,128)(2,1)S(1)}, u32[]{:S(2)}, u32[]{:S(2)}) async-start(bf16[16,288,2,8]{1,3,2,0:T(8,128)(2,1)} %copy.70), calls=%async_computation.2 | async-start | bytes 393216 | tf_op jit(solution)/shard_map/all_to_all | solution.py:107
  83.9 5.1 %all-to-all-done.2 = bf16[16,288,2,8]{1,3,2,0:T(8,128)(2,1)S(1)} async-done(((bf16[16,288,2,8]{1,3,2,0:T(8,128)(2,1)}), bf16[16,288,2,8]{1,3,2,0:T(8,128)(2,1)S(1)}, u32[]{:S(2)}, u32[]{:S(2)}) %all-to-all-start.2) | async-done | bytes 147488 | tf_op jit(solution)/shard_map/all_to_all | solution.py:107
  89.0 8.6 %fusion.8 = f32[2,4608,2,128]{1,3,0,2:T(8,128)S(1)} fusion(bf16[2,288,128,1]{1,2,3,0:T(8,128)(2,1)S(1)} %bitcast.82, bf16[2,2,288,4608]{3,2,1,0:T(8,128)(2,1)} %param.5, f32[2,288,4608]{2,1,0:T(8,128)} %mul.71), kind=kOutput, calls=%fused_computation.11 | convolution fusion | flops 1374879744 | bytes 30818304 | tf_op jit(solution)/shard_map/kfsn,fsc->knfc/dot_general | solution.py:112
  98.8 2.5 %pad_maximum_fusion = f32[4608,2,128]{0,2,1:T(8,128)} fusion(f32[4608,2,64]{0,2,1:T(8,128)S(1)} %get-tuple-element.6, f32[4608,2,64]{0,2,1:T(8,128)S(1)} %get-tuple-element.5), kind=kLoop, calls=%fused_computation.15 | loop fusion | flops 1179648 | bytes 9437184 | tf_op jit(solution)/shard_map/concatenate | solution.py:60
  101.3 8.1 %copy.75 = f32[4608,2,128]{2,1,0:T(2,128)} copy(f32[4608,2,128]{0,2,1:T(8,128)} %pad_maximum_fusion) | data formatting | bytes 9437184 | tf_op jit(solution)/shard_map/concatenate | solution.py:60
  109.3 92.7 %all-reduce.2 = bf16[4608,2,128]{2,1,0:T(2,128)(2,1)S(1)} all-reduce(f32[4608,2,128]{2,1,0:T(2,128)} %copy.75), channel_id=2, replica_groups=mesh['freq'=8,'rows'=16] {'rows'}, use_global_device_ids=true, to_apply=%region_0.1.clone | all-reduce | flops 1179648 | bytes 7077888
  202.5 9.4 %all_to_all.56 = bf16[288,2,2,64]{0,2,1,3:T(2,128)(2,1)S(1)} all-to-all(bf16[288,2,2,64]{0,2,1,3:T(2,128)(2,1)S(1)} %copy.77), channel_id=1, replica_groups=mesh['freq'=8,'rows'=16] {'freq'}, dimensions={3} | all-to-all | bytes 294912 | tf_op jit(solution)/shard_map/all_to_all | solution.py:117
  212.2 1.4 fusion.39
  213.7 1.4 convolution_add_fusion
  215.1 4.2 %fusion.3 = f32[8,288,1024]{2,1,0:T(8,128)} fusion(f32[8,288,1024]{2,1,0:T(8,128)S(1)} %bitcast.78, s32[8,288]{1,0:T(8,128)S(1)} %copy-done.2), kind=kLoop, calls=%fused_computation.6 | loop fusion | flops 4718592 | bytes 18883584 | tf_op jit(solution)/shard_map/jit(_where)/select_n | solution.py:125
  (34 shorter events, 5.8 us)
Async XLA Ops:
  0.0 30.3 %copy-start = (s32[288,64]{0,1:T(8,128)S(1)}, s32[288,64]{0,1:T(8,128)}, u32[]{:S(2)}) copy-start(s32[288,64]{0,1:T(8,128)} %param.8) | copy-start | bytes 221188
  2.8 39.8 %all-to-all-start = ((bf16[16,2,288,128]{3,2,1,0:T(8,128)(2,1)}), bf16[16,2,288,128]{3,2,1,0:T(8,128)(2,1)S(1)}, u32[]{:S(2)}, u32[]{:S(2)}) async-start(bf16[16,2,288,128]{3,2,1,0:T(8,128)(2,1)} %stack.2), calls=%async_computation | async-start | bytes 4718592 | tf_op jit(solution)/shard_map/all_to_all | solution.py:13
  52.8 11.6 %all-to-all-start.1 = ((bf16[2,288,2,64]{1,2,0,3:T(2,128)(2,1)}), bf16[2,288,2,64]{1,2,0,3:T(2,128)(2,1)S(1)}, u32[]{:S(2)}, u32[]{:S(2)}) async-start(bf16[2,288,2,64]{1,2,0,3:T(2,128)(2,1)} %copy.65), calls=%async_computation.1 | async-start | bytes 393216 | tf_op jit(solution)/shard_map/all_to_all | solution.py:94
  69.5 13.1 %copy-start.3 = (u32[128]{0:T(128)S(1)}, u32[128]{0:T(128)}, u32[]{:S(2)}) copy-start(u32[128]{0:T(128)} %constant.41) | copy-start | bytes 1540
  79.0 10.0 %all-to-all-start.2 = ((bf16[16,288,2,8]{1,3,2,0:T(8,128)(2,1)}), bf16[16,288,2,8]{1,3,2,0:T(8,128)(2,1)S(1)}, u32[]{:S(2)}, u32[]{:S(2)}) async-start(bf16[16,288,2,8]{1,3,2,0:T(8,128)(2,1)} %copy.70), calls=%async_computation.2 | async-start | bytes 393216 | tf_op jit(solution)/shard_map/all_to_all | solution.py:107
  213.7 1.4 copy-start.2
  215.1 4.2 %copy-start.1 = (s32[288,64]{0,1:T(8,128)S(1)}, s32[288,64]{0,1:T(8,128)}, u32[]{:S(2)}) copy-start(s32[288,64]{0,1:T(8,128)} %param.8) | copy-start | bytes 221188
